TPU v7x, 32 devices: a whole 2x2x4 slice. The times are simulated.
32 devices in a mesh: groups: 2 (over x), seq: 8 (over z, y), chan: 2 (over core).
Axes of the slice: x: 2, y: 2, z: 4, core: 2. Of those that a mesh axis runs over, the one named last changes fastest.
Arguments:
- query_proj: bfloat16 [16384, 256], P(('groups', 'seq'), 'chan'), parts along dimension 0, may hold values from -6 to 6
- key_proj: bfloat16 [16384, 256], P(('groups', 'seq'), 'chan'), parts along dimension 0, may hold values from -6 to 6
- value_proj: bfloat16 [16384, 256], P(('groups', 'seq'), 'chan'), parts along dimension 0, may hold values from -6 to 6
- long_filter: float32 [8192, 256], P('seq', 'chan'), may hold values from -4 to 4
- skip_bias: float32 [256], P('chan'), may hold values from -4 to 4
Outputs:
- gated_out: bfloat16 [16384, 256], P(('groups', 'seq'), 'chan'), parts along dimension 0
There are 2 independent parts, one for each index of `groups`. A program takes and returns all parts, laid end to end along the dimension named above; an argument that names none is the same for every part. Nothing has to cross between parts.
All inputs are finite; a program needn't handle non-finite values.
Results may differ from a plain program's by a relative error of at most 0.001.
Values sent between devices are 32-bit elements; how exact they have to be, the bound alone decides.
A program may use at most 64 MiB of HBM per device.

v0:
```python
import functools
import math

import jax
import jax.numpy as jnp
import numpy as np
from jax import lax
from jax.experimental import pallas as pl
from jax.experimental.pallas import tpu as pltpu
from jax.sharding import PartitionSpec as P

LANES = 128
SUB = 8
MESH = pl.DeviceIdType.MESH
F32 = jnp.float32
BF16 = jnp.bfloat16


def halves(table):
    high = table.astype(BF16)
    low = (table - high.astype(np.float64)).astype(BF16)
    return high, low


def tables(rows):
    length = rows * LANES
    quarter = np.arange(rows) + 0.25
    angle_a = 2.0 * math.pi / rows * np.outer(quarter, np.arange(rows))
    first = np.concatenate((np.cos(angle_a), -np.sin(angle_a)), axis=0)
    last = np.concatenate((np.cos(angle_a.T), -np.sin(angle_a.T)), axis=1) / length
    angle_t = 2.0 * math.pi / length * np.outer(quarter, np.arange(LANES))
    twist = np.stack((np.cos(angle_t), np.sin(angle_t))).astype(np.float32)
    angle_b = 2.0 * math.pi / LANES * (np.outer(np.arange(LANES), np.arange(LANES)) % LANES)
    cosine, sine = np.cos(angle_b), np.sin(angle_b)
    ahead = np.block([[cosine, -sine], [sine, cosine]])
    back = np.block([[cosine, sine], [-sine, cosine]])
    first_hi, first_lo = halves(first)
    last_hi, last_lo = halves(last)
    return (
        np.concatenate((first_hi, first_hi, first_lo), axis=1),
        np.concatenate((last_hi, last_hi, last_lo), axis=1),
        twist,
        np.stack(halves(ahead)),
        np.stack(halves(back)),
    )


def split(value):
    high = value.astype(BF16)
    return high, (value - high.astype(F32)).astype(BF16)


def dot(left, right):
    return jnp.dot(left, right, preferred_element_type=F32)


def times_table(value, table_ref):
    high, low = split(value)
    return dot(high, table_ref[0]) + dot(low, table_ref[0]) + dot(high, table_ref[1])


def table_times(table3, value):
    high, low = split(value)
    return dot(table3, jnp.concatenate((high, low, high), axis=0))


def body(n, groups, share, step, *refs):
    inputs, out_ref = refs[:10], refs[10]
    held = refs[11:21]
    (out_u, out_h, in_u, in_h, out_y, in_y, spec_h,
     send_sem, recv_sem, send_h_sem, recv_h_sem, own_sem, load_sem) = refs[21:]
    loads = [pltpu.make_async_copy(inputs[i], held[i], load_sem.at[i]) for i in range(10)]
    for i in (3, 1, 2, 5, 7, 8, 9, 6, 0, 4):
        loads[i].start()
    (q_ref, k_ref, v_ref, h_ref, skip_ref,
     first_ref, last_ref, twist_ref, ahead_ref, back_ref) = held
    me = lax.axis_index("seq")
    group = lax.axis_index("groups")
    part = share // groups
    blocks = k_ref.shape[0] // LANES
    rows = n * blocks
    chunks = share // step

    def peer_of(i):
        return lax.rem(me + i, n)

    barrier = pltpu.get_barrier_semaphore()

    def greet(i, carry):
        pl.semaphore_signal(barrier, inc=1, device_id={"seq": peer_of(i)}, device_id_type=MESH)
        return carry

    lax.fori_loop(1, n, greet, 0)
    for other in range(1, groups):
        pl.semaphore_signal(barrier, inc=1, device_id={"groups": lax.rem(group + other, groups)},
                            device_id_type=MESH)

    loads[3].wait()
    for a in range(blocks):
        tile = h_ref[pl.ds(a * LANES, LANES), :]
        out_h[pl.ds(a, LANES, stride=blocks), :] = tile.T
    pl.semaphore_wait(barrier, n + groups - 2)

    def slab(owner, j, width):
        return pl.ds(pl.multiple_of((owner * share + j * width) * blocks, SUB), width * blocks)

    def piece(owner, which):
        return pl.ds(pl.multiple_of((owner * share + which * part) * blocks, SUB), part * blocks)

    def h_copy(owner, sender, peer):
        return pltpu.make_async_remote_copy(
            src_ref=out_h.at[piece(owner, group)],
            dst_ref=in_h.at[sender, piece(0, group)],
            send_sem=send_h_sem.at[0, owner],
            recv_sem=recv_h_sem.at[0, sender],
            device_id={"seq": peer},
            device_id_type=MESH,
        )

    def h_pass(other, which, sender):
        return pltpu.make_async_remote_copy(
            src_ref=in_h.at[sender, piece(0, which)],
            dst_ref=in_h.at[sender, piece(0, which)],
            send_sem=send_h_sem.at[other, sender],
            recv_sem=recv_h_sem.at[other, sender],
            device_id={"groups": lax.rem(group + other, groups)},
            device_id_type=MESH,
        )

    def u_copy(j, owner, sender, peer):
        return pltpu.make_async_remote_copy(
            src_ref=out_u.at[slab(owner, j, step)],
            dst_ref=in_u.at[sender, slab(0, j, step)],
            send_sem=send_sem.at[0, j, owner],
            recv_sem=recv_sem.at[0, j, sender],
            device_id={"seq": peer},
            device_id_type=MESH,
        )

    def y_copy(j, owner, sender, peer):
        return pltpu.make_async_remote_copy(
            src_ref=out_y.at[owner, slab(0, j, step)],
            dst_ref=in_y.at[slab(sender, j, step)],
            send_sem=send_sem.at[1, j, owner],
            recv_sem=recv_sem.at[1, j, sender],
            device_id={"seq": peer},
            device_id_type=MESH,
        )

    def each_peer(act):
        def go(i, carry):
            act(peer_of(i))
            return carry

        lax.fori_loop(1, n, go, 0)

    each_peer(lambda p: h_copy(p, me, p).start())
    own_h = pltpu.make_async_copy(
        out_h.at[piece(me, group)], in_h.at[me, piece(0, group)], own_sem.at[0])
    own_h.start()

    loads[1].wait()
    loads[2].wait()
    for a in range(blocks):
        where = pl.ds(a * LANES, LANES)
        tile = k_ref[where, :].astype(F32) * v_ref[where, :].astype(F32)
        out_u[pl.ds(a, LANES, stride=blocks), :] = tile.T
    for j in range(chunks):
        each_peer(lambda p: u_copy(j, p, me, p).start())
    own_u = pltpu.make_async_copy(out_u.at[slab(me, 0, share)], in_u.at[me], own_sem.at[1])
    own_u.start()

    def forward(ref, j):
        parts = []
        for pair in range(0, step, 2):
            both = []
            for c in (pair, pair + 1):
                at = pl.ds(pl.multiple_of((j * step + c) * blocks, SUB), blocks)
                both.append(ref[:, at, :].reshape(rows, LANES))
            mixed = table_times(first_ref[...], jnp.concatenate(both, axis=1))
            for c in range(2):
                real = mixed[:rows, c * LANES:(c + 1) * LANES]
                imag = mixed[rows:, c * LANES:(c + 1) * LANES]
                cosine, sine = twist_ref[0], twist_ref[1]
                parts.append(jnp.concatenate(
                    (real * cosine + imag * sine, imag * cosine - real * sine), axis=1))
        return times_table(jnp.concatenate(parts, axis=0), ahead_ref)

    def pass_on(sender):
        for other in range(1, groups):
            h_pass(other, group, sender).start()

    def hand_on(sender):
        h_copy(me, sender, sender).wait_recv()
        pass_on(sender)

    own_h.wait()
    pass_on(me)
    each_peer(hand_on)
    for i in (5, 7, 8):
        loads[i].wait()

    def receive(sender, carry):
        for other in range(1, groups):
            h_pass(other, lax.rem(group + groups - other, groups), sender).wait_recv()
        return carry

    lax.fori_loop(0, n, receive, 0)

    def filter_step(j, carry):
        spec_h[j] = forward(in_h, j)
        return carry

    lax.fori_loop(0, chunks, filter_step, 0)
    own_u.wait()
    loads[6].wait()
    loads[9].wait()

    def chunk_step(j, carry):
        each_peer(lambda p: u_copy(j, me, p, p).wait_recv())
        spec = forward(in_u, j)
        other = spec_h[j]
        ur, ui = spec[:, :LANES], spec[:, LANES:]
        hr, hi = other[:, :LANES], other[:, LANES:]
        prod = jnp.concatenate((ur * hr - ui * hi, ur * hi + ui * hr), axis=1)
        turned = times_table(prod, back_ref)
        for pair in range(0, step, 2):
            both = []
            for c in (pair, pair + 1):
                real = turned[c * rows:(c + 1) * rows, :LANES]
                imag = turned[c * rows:(c + 1) * rows, LANES:]
                cosine, sine = twist_ref[0], twist_ref[1]
                both.append(jnp.concatenate(
                    (real * cosine - imag * sine, real * sine + imag * cosine), axis=0))
            result = table_times(last_ref[...], jnp.concatenate(both, axis=1))
            for c in range(2):
                at = pl.ds(pl.multiple_of((j * step + pair + c) * blocks, SUB), blocks)
                out_y[:, at, :] = result[:, c * LANES:(c + 1) * LANES].reshape(n, blocks, LANES)
        each_peer(lambda p: y_copy(j, p, me, p).start())
        return carry

    lax.fori_loop(0, chunks, chunk_step, 0)
    own_y = pltpu.make_async_copy(out_y.at[me], in_y.at[slab(me, 0, share)], own_sem.at[2])
    own_y.start()
    own_y.wait()
    loads[0].wait()
    loads[4].wait()
    for j in range(chunks):
        each_peer(lambda p: y_copy(j, me, p, p).wait_recv())

    for a in range(blocks):
        where = pl.ds(a * LANES, LANES)
        driver = k_ref[where, :].astype(F32) * v_ref[where, :].astype(F32)
        conv = in_y[pl.ds(a, LANES, stride=blocks), :].T
        out_ref[where, :] = (
            q_ref[where, :].astype(F32) * (conv + skip_ref[...] * driver)
        ).astype(BF16)

    each_peer(lambda p: h_copy(p, me, p).wait_send())

    def passed(sender, carry):
        for other in range(1, groups):
            h_pass(other, group, sender).wait_send()
        return carry

    lax.fori_loop(0, n, passed, 0)
    for j in range(chunks):
        each_peer(lambda p: u_copy(j, p, me, p).wait_send())
        each_peer(lambda p: y_copy(j, p, me, p).wait_send())


def shards(n, groups, query_proj, key_proj, value_proj, long_filter, skip_bias):
    tokens, chans = key_proj.shape
    share = chans // n
    step = min(8, share)
    chunks = share // step
    blocks = tokens // LANES
    rows = n * blocks
    operands = (
        query_proj, key_proj, value_proj, long_filter, skip_bias.reshape(1, chans), *tables(rows))
    return pl.pallas_call(
        functools.partial(body, n, groups, share, step),
        out_shape=jax.ShapeDtypeStruct((tokens, chans), BF16),
        in_specs=[pl.BlockSpec(memory_space=pltpu.HBM)] * len(operands),
        out_specs=pl.BlockSpec(memory_space=pltpu.VMEM),
        scratch_shapes=[pltpu.VMEM(x.shape, x.dtype) for x in operands] + [
            pltpu.VMEM((chans * blocks, LANES), F32),
            pltpu.VMEM((chans * blocks, LANES), F32),
            pltpu.VMEM((n, share * blocks, LANES), F32),
            pltpu.VMEM((n, share * blocks, LANES), F32),
            pltpu.VMEM((n, share * blocks, LANES), F32),
            pltpu.VMEM((chans * blocks, LANES), F32),
            pltpu.VMEM((chunks, step * rows, 2 * LANES), F32),
            pltpu.SemaphoreType.DMA((2, chunks, n)),
            pltpu.SemaphoreType.DMA((2, chunks, n)),
            pltpu.SemaphoreType.DMA((groups, n)),
            pltpu.SemaphoreType.DMA((groups, n)),
            pltpu.SemaphoreType.DMA((3,)),
            pltpu.SemaphoreType.DMA((len(operands),)),
        ],
        compiler_params=pltpu.CompilerParams(
            collective_id=0, has_side_effects=True, vmem_limit_bytes=48 * 1024 * 1024
        ),
        name="hyena_conv",
    )(*[pltpu.with_memory_space_constraint(x, pltpu.HBM) for x in operands])


def solution(mesh):
    placed = (
        P(("groups", "seq"), "chan"),
        P(("groups", "seq"), "chan"),
        P(("groups", "seq"), "chan"),
        P("seq", "chan"),
        P("chan"),
    )
    return jax.shard_map(
        functools.partial(shards, mesh.shape["seq"], mesh.shape["groups"]),
        mesh=mesh,
        in_specs=placed,
        out_specs=P(("groups", "seq"), "chan"),
        check_vma=False,
    )
```

profile of v0, /device:TPU:0, one launch (start us, length us, event | category | flops | bytes accessed | tf_op | source)
XLA Modules:
  0.0 36.3 jit_solution(15223805251896379031)
XLA Ops:
  0.0 35.6 %hyena_conv.1 = bf16[1024,128]{1,0:T(8,128)(2,1)S(1)} custom-call(bf16[1024,128]{1,0:T(8,128)(2,1)} %refs_0_.1, bf16[1024,128]{1,0:T(8,128)(2,1)} %refs_1_.1, bf16[1024,128]{1,0:T(8,128)(2,1)} %refs_2_.1, f32[1024,128]{1,0:T(8,128)} %refs_3_.1, f32[1,128]{1,0:T(1,128)} %bitcast.1, bf16[128,192]{1,0:T(8,128)(2,1)} %constant.10.clone.refs_5_, ...), custom_call_target="tpu_custom_call" | custom-call | tf_op jit(solution)/shard_map/hyena_conv/pallas_call | solution.py:281
  35.6 0.7 %copy.12 = bf16[1024,128]{1,0:T(8,128)(2,1)} copy(bf16[1024,128]{1,0:T(8,128)(2,1)S(1)} %hyena_conv.1) | data formatting | bytes 524288
where the time goes:
time: 36.5 us; the launch traced here: 36.3 us
  Pallas kernels  35.6 us (98%)
  local copies, waits for them, and re-layouts  0.71 us (2%)
    pallas_call x1, Pallas kernels, shards(): pl.pallas_call(functools.partial(body, n, groups, share, step), out_shape...  35.6 us

commit v1 on v0

--- a/solution.py
+++ b/solution.py
@@ -11,6 +11,7 @@
 
 LANES = 128
 SUB = 8
+UNROLL = 8
 MESH = pl.DeviceIdType.MESH
 F32 = jnp.float32
 BF16 = jnp.bfloat16
@@ -68,7 +69,7 @@
     inputs, out_ref = refs[:10], refs[10]
     held = refs[11:21]
     (out_u, out_h, in_u, in_h, out_y, in_y, spec_h,
-     send_sem, recv_sem, send_h_sem, recv_h_sem, own_sem, load_sem) = refs[21:]
+     send_sem, recv_u_sem, recv_h_sem, recv_sem, own_sem, load_sem) = refs[21:]
     loads = [pltpu.make_async_copy(inputs[i], held[i], load_sem.at[i]) for i in range(10)]
     for i in (3, 1, 2, 5, 7, 8, 9, 6, 0, 4):
         loads[i].start()
@@ -81,18 +82,34 @@
     rows = n * blocks
     chunks = share // step
 
+    def wrap(i, size):
+        return jnp.where(i >= size, i - size, i)
+
     def peer_of(i):
-        return lax.rem(me + i, n)
+        return wrap(me + i, n)
+
+    def each_peer(act):
+        if n <= UNROLL:
+            for i in range(1, n):
+                act(peer_of(i))
+            return
+
+        def go(i, carry):
+            act(peer_of(i))
+            return carry
+
+        lax.fori_loop(1, n, go, 0)
+
+    def drain(ref, height, sem):
+        where = ref.at[pl.ds(0, height)]
+        pltpu.make_async_copy(where, where, sem).wait()
 
     barrier = pltpu.get_barrier_semaphore()
 
-    def greet(i, carry):
-        pl.semaphore_signal(barrier, inc=1, device_id={"seq": peer_of(i)}, device_id_type=MESH)
-        return carry
-
-    lax.fori_loop(1, n, greet, 0)
+    each_peer(lambda p: pl.semaphore_signal(
+        barrier, inc=1, device_id={"seq": p}, device_id_type=MESH))
     for other in range(1, groups):
-        pl.semaphore_signal(barrier, inc=1, device_id={"groups": lax.rem(group + other, groups)},
+        pl.semaphore_signal(barrier, inc=1, device_id={"groups": wrap(group + other, groups)},
                             device_id_type=MESH)
 
     loads[3].wait()
@@ -111,8 +128,8 @@
         return pltpu.make_async_remote_copy(
             src_ref=out_h.at[piece(owner, group)],
             dst_ref=in_h.at[sender, piece(0, group)],
-            send_sem=send_h_sem.at[0, owner],
-            recv_sem=recv_h_sem.at[0, sender],
+            send_sem=send_sem.at[0],
+            recv_sem=recv_h_sem.at[sender],
             device_id={"seq": peer},
             device_id_type=MESH,
         )
@@ -121,9 +138,9 @@
         return pltpu.make_async_remote_copy(
             src_ref=in_h.at[sender, piece(0, which)],
             dst_ref=in_h.at[sender, piece(0, which)],
-            send_sem=send_h_sem.at[other, sender],
-            recv_sem=recv_h_sem.at[other, sender],
-            device_id={"groups": lax.rem(group + other, groups)},
+            send_sem=send_sem.at[1],
+            recv_sem=recv_sem.at[0],
+            device_id={"groups": wrap(group + other, groups)},
             device_id_type=MESH,
         )
 
@@ -131,8 +148,8 @@
         return pltpu.make_async_remote_copy(
             src_ref=out_u.at[slab(owner, j, step)],
             dst_ref=in_u.at[sender, slab(0, j, step)],
-            send_sem=send_sem.at[0, j, owner],
-            recv_sem=recv_sem.at[0, j, sender],
+            send_sem=send_sem.at[2],
+            recv_sem=recv_u_sem.at[j],
             device_id={"seq": peer},
             device_id_type=MESH,
         )
@@ -141,22 +158,15 @@
         return pltpu.make_async_remote_copy(
             src_ref=out_y.at[owner, slab(0, j, step)],
             dst_ref=in_y.at[slab(sender, j, step)],
-            send_sem=send_sem.at[1, j, owner],
-            recv_sem=recv_sem.at[1, j, sender],
+            send_sem=send_sem.at[3],
+            recv_sem=recv_sem.at[1],
             device_id={"seq": peer},
             device_id_type=MESH,
         )
 
-    def each_peer(act):
-        def go(i, carry):
-            act(peer_of(i))
-            return carry
-
-        lax.fori_loop(1, n, go, 0)
-
     each_peer(lambda p: h_copy(p, me, p).start())
     own_h = pltpu.make_async_copy(
-        out_h.at[piece(me, group)], in_h.at[me, piece(0, group)], own_sem.at[0])
+        out_h.at[slab(me, 0, share)], in_h.at[me], own_sem.at[0])
     own_h.start()
 
     loads[1].wait()
@@ -194,18 +204,12 @@
         h_copy(me, sender, sender).wait_recv()
         pass_on(sender)
 
+    each_peer(hand_on)
     own_h.wait()
-    pass_on(me)
-    each_peer(hand_on)
     for i in (5, 7, 8):
         loads[i].wait()
 
-    def receive(sender, carry):
-        for other in range(1, groups):
-            h_pass(other, lax.rem(group + groups - other, groups), sender).wait_recv()
-        return carry
-
-    lax.fori_loop(0, n, receive, 0)
+    drain(out_h, (groups - 1) * (n - 1) * part * blocks, recv_sem.at[0])
 
     def filter_step(j, carry):
         spec_h[j] = forward(in_h, j)
@@ -217,7 +221,8 @@
     loads[9].wait()
 
     def chunk_step(j, carry):
-        each_peer(lambda p: u_copy(j, me, p, p).wait_recv())
+        arrived = in_u.at[pl.ds(0, n - 1), slab(0, j, step)]
+        pltpu.make_async_copy(arrived, arrived, recv_u_sem.at[j]).wait()
         spec = forward(in_u, j)
         other = spec_h[j]
         ur, ui = spec[:, :LANES], spec[:, LANES:]
@@ -245,8 +250,10 @@
     own_y.wait()
     loads[0].wait()
     loads[4].wait()
-    for j in range(chunks):
-        each_peer(lambda p: y_copy(j, me, p, p).wait_recv())
+    drain(out_h, (n - 1) * part * blocks, send_sem.at[0])
+    drain(out_h, (groups - 1) * (n - 1) * part * blocks, send_sem.at[1])
+    drain(out_u, (n - 1) * share * blocks, send_sem.at[2])
+    drain(in_y, (n - 1) * share * blocks, recv_sem.at[1])
 
     for a in range(blocks):
         where = pl.ds(a * LANES, LANES)
@@ -256,17 +263,7 @@
             q_ref[where, :].astype(F32) * (conv + skip_ref[...] * driver)
         ).astype(BF16)
 
-    each_peer(lambda p: h_copy(p, me, p).wait_send())
-
-    def passed(sender, carry):
-        for other in range(1, groups):
-            h_pass(other, group, sender).wait_send()
-        return carry
-
-    lax.fori_loop(0, n, passed, 0)
-    for j in range(chunks):
-        each_peer(lambda p: u_copy(j, p, me, p).wait_send())
-        each_peer(lambda p: y_copy(j, p, me, p).wait_send())
+    drain(in_y, (n - 1) * share * blocks, send_sem.at[3])
 
 
 def shards(n, groups, query_proj, key_proj, value_proj, long_filter, skip_bias):
@@ -291,10 +288,10 @@
             pltpu.VMEM((n, share * blocks, LANES), F32),
             pltpu.VMEM((chans * blocks, LANES), F32),
             pltpu.VMEM((chunks, step * rows, 2 * LANES), F32),
-            pltpu.SemaphoreType.DMA((2, chunks, n)),
-            pltpu.SemaphoreType.DMA((2, chunks, n)),
-            pltpu.SemaphoreType.DMA((groups, n)),
-            pltpu.SemaphoreType.DMA((groups, n)),
+            pltpu.SemaphoreType.DMA((4,)),
+            pltpu.SemaphoreType.DMA((chunks,)),
+            pltpu.SemaphoreType.DMA((n,)),
+            pltpu.SemaphoreType.DMA((2,)),
             pltpu.SemaphoreType.DMA((3,)),
             pltpu.SemaphoreType.DMA((len(operands),)),
         ],

time: 36.5 us -> 35.4 us (0.970)
  Pallas kernels: 35.6 us -> 34.5 us
    pallas_call x1, Pallas kernels: 35.6 us -> 34.5 us  [shards(): pl.pallas_call(functools.partial(body, n, groups, share, step), out_shape...]
where the time goes in v1:
time: 35.4 us; the launch traced here: 35.2 us
  Pallas kernels  34.5 us (97%)
  local copies, waits for them, and re-layouts  0.71 us (2%)
    pallas_call x1, Pallas kernels, shards(): pl.pallas_call(functools.partial(body, n, groups, share, step), out_shape...  34.5 us

profile of v1, /device:TPU:0, one launch (start us, length us, event | category | flops | bytes accessed | tf_op | source)
XLA Modules:
  0.0 35.2 jit_solution(13599601575134671130)
XLA Ops:
  0.0 34.5 %hyena_conv.1 = bf16[1024,128]{1,0:T(8,128)(2,1)S(1)} custom-call(bf16[1024,128]{1,0:T(8,128)(2,1)} %refs_0_.1, bf16[1024,128]{1,0:T(8,128)(2,1)} %refs_1_.1, bf16[1024,128]{1,0:T(8,128)(2,1)} %refs_2_.1, f32[1024,128]{1,0:T(8,128)} %refs_3_.1, f32[1,128]{1,0:T(1,128)} %bitcast.1, bf16[128,192]{1,0:T(8,128)(2,1)} %constant.10.clone.refs_5_, ...), custom_call_target="tpu_custom_call" | custom-call | tf_op jit(solution)/shard_map/hyena_conv/pallas_call | solution.py:278
  34.5 0.7 %copy.12 = bf16[1024,128]{1,0:T(8,128)(2,1)} copy(bf16[1024,128]{1,0:T(8,128)(2,1)S(1)} %hyena_conv.1) | data formatting | bytes 524288

commit v2 on v1

--- a/solution.py
+++ b/solution.py
@@ -88,14 +88,14 @@
     def peer_of(i):
         return wrap(me + i, n)
 
-    def each_peer(act):
+    def each_peer(act, back=False):
         if n <= UNROLL:
             for i in range(1, n):
-                act(peer_of(i))
+                act(peer_of(n - i if back else i))
             return
 
         def go(i, carry):
-            act(peer_of(i))
+            act(peer_of(n - i if back else i))
             return carry
 
         lax.fori_loop(1, n, go, 0)
@@ -176,7 +176,7 @@
         tile = k_ref[where, :].astype(F32) * v_ref[where, :].astype(F32)
         out_u[pl.ds(a, LANES, stride=blocks), :] = tile.T
     for j in range(chunks):
-        each_peer(lambda p: u_copy(j, p, me, p).start())
+        each_peer(lambda p: u_copy(j, p, me, p).start(), back=True)
     own_u = pltpu.make_async_copy(out_u.at[slab(me, 0, share)], in_u.at[me], own_sem.at[1])
     own_u.start()
 

time: 35.4 us -> 34.9 us (0.986)
  Pallas kernels: 34.5 us -> 34 us
    pallas_call x1, Pallas kernels: 34.5 us -> 34 us  [shards(): pl.pallas_call(functools.partial(body, n, groups, share, step), out_shape...]
where the time goes in v2:
time: 34.9 us; the launch traced here: 34.8 us
  Pallas kernels  34 us (97%)
  local copies, waits for them, and re-layouts  0.71 us (2%)
    pallas_call x1, Pallas kernels, shards(): pl.pallas_call(functools.partial(body, n, groups, share, step), out_shape...  34 us
    unnamed x1, local copies, waits for them, and re-layouts  0.71 us

profile of v2, /device:TPU:0, one launch (start us, length us, event | category | flops | bytes accessed | tf_op | source)
XLA Modules:
  0.0 34.8 jit_solution(9507334533995582705)
XLA Ops:
  0.0 34.0 %hyena_conv.1 = bf16[1024,128]{1,0:T(8,128)(2,1)S(1)} custom-call(bf16[1024,128]{1,0:T(8,128)(2,1)} %refs_0_.1, bf16[1024,128]{1,0:T(8,128)(2,1)} %refs_1_.1, bf16[1024,128]{1,0:T(8,128)(2,1)} %refs_2_.1, f32[1024,128]{1,0:T(8,128)} %refs_3_.1, f32[1,128]{1,0:T(1,128)} %bitcast.1, bf16[128,192]{1,0:T(8,128)(2,1)} %constant.10.clone.refs_5_, ...), custom_call_target="tpu_custom_call" | custom-call | tf_op jit(solution)/shard_map/hyena_conv/pallas_call | solution.py:278
  34.0 0.7 %copy.12 = bf16[1024,128]{1,0:T(8,128)(2,1)} copy(bf16[1024,128]{1,0:T(8,128)(2,1)S(1)} %hyena_conv.1) | data formatting | bytes 524288

commit v3 on v2

--- a/solution.py
+++ b/solution.py
@@ -107,7 +107,7 @@
     barrier = pltpu.get_barrier_semaphore()
 
     each_peer(lambda p: pl.semaphore_signal(
-        barrier, inc=1, device_id={"seq": p}, device_id_type=MESH))
+        barrier, inc=1, device_id={"seq": p}, device_id_type=MESH), back=True)
     for other in range(1, groups):
         pl.semaphore_signal(barrier, inc=1, device_id={"groups": wrap(group + other, groups)},
                             device_id_type=MESH)
@@ -247,13 +247,13 @@
     lax.fori_loop(0, chunks, chunk_step, 0)
     own_y = pltpu.make_async_copy(out_y.at[me], in_y.at[slab(me, 0, share)], own_sem.at[2])
     own_y.start()
-    own_y.wait()
     loads[0].wait()
     loads[4].wait()
     drain(out_h, (n - 1) * part * blocks, send_sem.at[0])
     drain(out_h, (groups - 1) * (n - 1) * part * blocks, send_sem.at[1])
     drain(out_u, (n - 1) * share * blocks, send_sem.at[2])
     drain(in_y, (n - 1) * share * blocks, recv_sem.at[1])
+    own_y.wait()
 
     for a in range(blocks):
         where = pl.ds(a * LANES, LANES)

time: 34.9 us -> 34.9 us (level)
  no operation moved by 1% of the time
where the time goes in v3:
time: 34.9 us; the launch traced here: 34.7 us
  Pallas kernels  34 us (97%)
  local copies, waits for them, and re-layouts  0.71 us (2%)
    pallas_call x1, Pallas kernels, shards(): pl.pallas_call(functools.partial(body, n, groups, share, step), out_shape...  34 us
    unnamed x1, local copies, waits for them, and re-layouts  0.71 us

profile of v3, /device:TPU:0, one launch (start us, length us, event | category | flops | bytes accessed | tf_op | source)
XLA Modules:
  0.0 34.7 jit_solution(15643059997360714527)
XLA Ops:
  0.0 34.0 %hyena_conv.1 = bf16[1024,128]{1,0:T(8,128)(2,1)S(1)} custom-call(bf16[1024,128]{1,0:T(8,128)(2,1)} %refs_0_.1, bf16[1024,128]{1,0:T(8,128)(2,1)} %refs_1_.1, bf16[1024,128]{1,0:T(8,128)(2,1)} %refs_2_.1, f32[1024,128]{1,0:T(8,128)} %refs_3_.1, f32[1,128]{1,0:T(1,128)} %bitcast.1, bf16[128,192]{1,0:T(8,128)(2,1)} %constant.10.clone.refs_5_, ...), custom_call_target="tpu_custom_call" | custom-call | tf_op jit(solution)/shard_map/hyena_conv/pallas_call | solution.py:278
  34.0 0.7 %copy.12 = bf16[1024,128]{1,0:T(8,128)(2,1)} copy(bf16[1024,128]{1,0:T(8,128)(2,1)S(1)} %hyena_conv.1) | data formatting | bytes 524288
